TPU v7x, 256 devices: a whole 4x4x8 slice. The times are simulated.
256 devices in a mesh: dom: 128 (over z, y, x), ord: 2 (over core).
Axes of the slice: x: 4, y: 4, z: 8, core: 2. Of those that a mesh axis runs over, the one named last changes fastest.
Arguments:
- polar_images: bfloat16 [1024, 128, 512], P(('dom', 'ord')), may hold values from -6 to 6
- radial_basis: bfloat16 [256, 128, 128], P('ord'), may hold values from -0.5 to 0.5
- radial_start: int32 [256], P('ord'), may hold values from 0 to 4, as said below
- radial_count: int32 [256], P('ord'), may hold values from 32 to 128
- order_of_slot: int32 [256], replicated, may hold values from 0 to 255, each once
- start_block: float32 [256, 16, 128], P('ord'), may hold values from -6 to 6
Outputs:
- denoised: bfloat16 [1024, 128, 512], P(('dom', 'ord'))
Inputs may be any that keep to these rules, and one draw needn't show every extreme that they name: `radial_start`: every slot keeps at least 64 radial samples.
All inputs are finite; a program needn't handle non-finite values.
Results may differ from a plain program's by a relative error of at most 0.01.
Values may be sent and summed in bfloat16 or wider, within the bound.
A program may use at most 64 MiB of HBM per device.

v0:
```python
import math
import jax
import jax.numpy as jnp
from jax import lax
from jax.sharding import PartitionSpec as P

NRB = 8
ITERS = 4


def make_table(order_of_slot, angles):
    steps_t = jnp.arange(angles, dtype=jnp.int32)
    phase_int = steps_t[:, None] * order_of_slot[None, :] % angles
    radians = phase_int.astype(jnp.float32) * (2.0 * math.pi / angles)
    weight = math.sqrt(2.0 / angles)
    paired = jnp.stack([jnp.cos(radians) * weight, -jnp.sin(radians) * weight], axis=2)
    return paired.reshape(angles, -1).astype(jnp.bfloat16)


def masked_basis(radial_basis, radial_start, radial_count, blocks):
    radial_rows = radial_basis.shape[1]
    slot_cols = radial_basis.shape[2]
    row_ids = jnp.arange(radial_rows, dtype=jnp.int32)
    col_ids = jnp.arange(slot_cols, dtype=jnp.int32)
    keep_rows = row_ids[None, :, None] >= radial_start[:, None, None] * (radial_rows // blocks)
    keep_cols = col_ids[None, None, :] < radial_count[:, None, None]
    return jnp.where(keep_rows & keep_cols, radial_basis, jnp.zeros_like(radial_basis))


def orthonormal(image_t):
    gram_matrix = jnp.einsum("srq,stq->srt", image_t, image_t, precision=lax.Precision.HIGHEST)
    factor = jnp.linalg.cholesky(gram_matrix)
    return jax.scipy.linalg.solve_triangular(factor, image_t, lower=True)


def subspace(cov_mat, start_t):
    basis_t = start_t
    for step in range(ITERS):
        image_t = jnp.einsum("srm,smq->srq", basis_t, cov_mat, precision=lax.Precision.HIGHEST)
        basis_t = orthonormal(image_t)
    return basis_t


def radial_images(eig_t, masked):
    return jnp.einsum("stq,srq->str", eig_t, masked, preferred_element_type=jnp.float32).astype(
        jnp.bfloat16
    )


def on_device(polar_images, radial_basis, radial_start, radial_count, order_of_slot, start_block):
    particles, radial_rows, angles = polar_images.shape
    dft_table = make_table(order_of_slot, angles)
    spectrum = jnp.dot(
        polar_images.reshape(particles * radial_rows, angles),
        dft_table,
        preferred_element_type=jnp.float32,
    )
    spectrum = spectrum.astype(jnp.bfloat16).reshape(particles, radial_rows, -1)
    regrouped = lax.all_to_all(spectrum, "ord", split_axis=2, concat_axis=0, tiled=True)
    owned_slots = radial_basis.shape[0]
    group_rows = regrouped.shape[0]
    local_spec = regrouped.reshape(group_rows, radial_rows, owned_slots, 2)
    masked = masked_basis(radial_basis, radial_start, radial_count, NRB)
    coef_four = jnp.einsum(
        "prsc,srq->scpq", local_spec, masked, preferred_element_type=jnp.float32
    ).astype(jnp.bfloat16)
    coef_rows = coef_four.reshape(owned_slots, 2 * group_rows, -1)
    partial_value = jnp.einsum(
        "snq,snm->sqm", coef_rows, coef_rows, preferred_element_type=jnp.float32
    )
    cov_mine = lax.psum_scatter(partial_value, "dom", scatter_dimension=0, tiled=True)
    share_count = cov_mine.shape[0]
    first_slot = lax.axis_index("dom") * share_count
    mine_start = lax.dynamic_slice_in_dim(start_block, first_slot, share_count, 0)
    mine_basis = lax.dynamic_slice_in_dim(masked, first_slot, share_count, 0)
    eig_mine = subspace(cov_mine, mine_start).astype(jnp.bfloat16)
    u_mine = radial_images(eig_mine, mine_basis)
    eig_t, u_t = (
        lax.all_gather(eig_mine, "dom", axis=0, tiled=True),
        lax.all_gather(u_mine, "dom", axis=0, tiled=True),
    )
    scores = jnp.einsum(
        "scpq,stq->psct", coef_four, eig_t, preferred_element_type=jnp.float32
    ).astype(jnp.bfloat16)
    local_profile = jnp.einsum(
        "psct,str->prsc", scores, u_t, preferred_element_type=jnp.float32
    ).astype(jnp.bfloat16)
    local_profile = local_profile.reshape(group_rows, radial_rows, -1)
    profile = lax.all_to_all(local_profile, "ord", split_axis=0, concat_axis=2, tiled=True).reshape(
        particles * radial_rows, -1
    )
    denoised = lax.dot_general(
        profile, dft_table, (((1,), (1,)), ((), ())), preferred_element_type=jnp.float32
    )
    return denoised.astype(jnp.bfloat16).reshape(particles, radial_rows, angles)


def solution(mesh):
    placed = (
        P(("dom", "ord"), None, None),
        P("ord", None, None),
        P("ord"),
        P("ord"),
        P(),
        P("ord", None, None),
    )
    return jax.shard_map(
        on_device,
        mesh=mesh,
        in_specs=placed,
        out_specs=P(("dom", "ord"), None, None),
        check_vma=False,
    )
```

profile of v0, /device:TPU:1, one launch (start us, length us, event | category | flops | bytes accessed | tf_op | source)
XLA Modules:
  0.0 1476.3 jit_solution(6241815372960781831)
XLA Ops:
  6.5 3.0 multiply_convert_fusion.1
  10.4 1.5 convolution_convert_fusion.3
  11.9 1.1 copy.49
  13.0 6.7 all-to-all-start
  19.6 1.4 all-to-all-done
  21.3 6.0 and_select_fusion
  27.4 2.0 copy-done.1
  29.3 1.2 fusion.2
  30.5 4.5 fusion.12
  35.1 620.3 %reduce-scatter.2.cloned.1.call-done = f32[1,128,128]{2,1,0:T(8,128)} async-done(((f32[128,128,128]{2,1,0:T(8,128)}), f32[1,128,128]{2,1,0:T(8,128)}) %reduce-scatter.2.cloned.1.call-update) | async-done | bytes 65552 | tf_op jit(solution)/shard_map/reduce_scatter | solution.py:71
  655.4 1.0 fusion.25
  656.6 1.5 custom-call.12
  658.8 0.6 select_select_fusion.3
  659.4 1.2 custom-call.13
  660.8 1.0 fusion.23
  662.1 1.5 custom-call.14
  664.2 0.6 select_select_fusion.2
  664.9 1.2 custom-call.15
  666.3 1.0 fusion.21
  667.5 1.5 custom-call.16
  669.7 0.6 select_select_fusion.1
  670.3 1.2 custom-call.17
  671.8 1.0 fusion.19
  673.0 1.5 custom-call.18
  675.8 1.2 custom-call.19
  677.2 0.9 convolution_convert_fusion.4
  678.1 287.7 %all_gather.7 = bf16[128,16,128]{2,1,0:T(8,128)(2,1)S(1)} all-gather(bf16[1,16,128]{2,1,0:T(8,128)(2,1)S(1)} %fusion.6), channel_id=1, replica_groups=mesh['dom'=128,'ord'=2] {'dom'}, dimensions={0}, use_global_device_ids=true | all-gather | bytes 528384 | tf_op jit(solution)/shard_map/all_gather | solution.py:79
  965.9 285.6 %all-gather = bf16[2048,128]{1,0:T(8,128)(2,1)S(1)} all-gather(bf16[16,128]{1,0:T(8,128)(2,1)S(1)} %convolution_convert_fusion.4), channel_id=2, replica_groups=mesh['dom'=128,'ord'=2] {'dom'}, dimensions={0}, use_global_device_ids=true | all-gather | bytes 528384 | tf_op jit(solution)/shard_map/all_gather | solution.py:80
  1251.4 1.3 convolution_convert_fusion.1
  1252.7 1.3 copy.59
  1254.1 213.6 %all_to_all.30 = bf16[8,128,256]{2,1,0:T(8,128)(2,1)S(1)} all-to-all(bf16[8,128,256]{2,1,0:T(8,128)(2,1)S(1)} %copy.59), channel_id=1, replica_groups=mesh['dom'=128,'ord'=2] {'ord'}, dimensions={0} | all-to-all | bytes 1048576 | tf_op jit(solution)/shard_map/all_to_all | solution.py:89
  1468.3 1.2 convolution_convert_fusion
  (42 shorter events, 6.8 us)
Async XLA Ops:
  6.5 648.9 %copy-start = (f32[128,16,128]{2,1,0:T(8,128)S(1)}, f32[128,16,128]{2,1,0:T(8,128)}, u32[]{:S(2)}) copy-start(f32[128,16,128]{2,1,0:T(8,128)} %param.14) | copy-start | bytes 3145732
  6.5 13.1 copy-start.3
  6.5 14.7 copy-start.2
  13.0 8.1 all-to-all-start
  19.6 635.7 %reduce-scatter.2.cloned.1.call-start = ((), (), s32[]{:S(2)}) async-start(), calls=%async_computation.3 | async-start | bytes 8454144 | tf_op jit(solution)/shard_map/reduce_scatter | solution.py:71
  27.4 2.0 copy-start.1
Sparse Core Ops, SparseCore 0:
  35.2 620.1 reduce-scatter.1
where the time goes:
time: 1480 us
  blocking collectives  787 us (53%)
  waiting for transfers between devices  622 us (42%)
  other arithmetic  25.4 us (2%)
  matrix products  16.1 us (1%)
    reduce_scatter x1, waiting for transfers between devices, on_device(): lax.psum_scatter(partial_value, 'dom', scatter_dimension=0, tiled=True)  620 us
    all_gather x1, blocking collectives, on_device(): lax.all_gather(eig_mine, 'dom', axis=0, tiled=True)  288 us
    all_gather x1, blocking collectives, on_device(): lax.all_gather(u_mine, 'dom', axis=0, tiled=True)  286 us
    all_to_all x1, blocking collectives, on_device(): lax.all_to_all(local_profile, 'ord', split_axis=0, concat_axis=2, tiled=T...  214 us
  transfers between devices with their start and end apart: 2, of which 2 were waited for; matrix products, arithmetic and copies ran while one was open for 0% of the time, Pallas kernels for 0%

commit v1 on v0

--- a/solution.py
+++ b/solution.py
@@ -1,3 +1,4 @@
+import functools
 import math
 import jax
 import jax.numpy as jnp
@@ -6,6 +7,19 @@
 
 NRB = 8
 ITERS = 4
+
+
+def cut_sources_all(message, mesh_ax):
+    fields = []
+    for _ in range(jax.lax.axis_size(mesh_ax)):
+        fields.append(message)
+    return jnp.concatenate(
+        jax.lax.all_to_all(jnp.stack(fields), axis_name=mesh_ax, split_axis=0, concat_axis=0),
+        axis=0,
+    )
+
+
+rest_the_rates = functools.partial(cut_sources_all, mesh_ax="dom")
 
 
 def make_table(order_of_slot, angles):
@@ -75,10 +89,7 @@
     mine_basis = lax.dynamic_slice_in_dim(masked, first_slot, share_count, 0)
     eig_mine = subspace(cov_mine, mine_start).astype(jnp.bfloat16)
     u_mine = radial_images(eig_mine, mine_basis)
-    eig_t, u_t = (
-        lax.all_gather(eig_mine, "dom", axis=0, tiled=True),
-        lax.all_gather(u_mine, "dom", axis=0, tiled=True),
-    )
+    eig_t, u_t = (rest_the_rates(eig_mine), lax.all_gather(u_mine, "dom", axis=0, tiled=True))
     scores = jnp.einsum(
         "scpq,stq->psct", coef_four, eig_t, preferred_element_type=jnp.float32
     ).astype(jnp.bfloat16)

time: 1480 us -> 1150 us (0.78)
  blocking collectives: 787 us -> 453 us
    all_gather x1 -> x0, blocking collectives: 288 us -> none  [on_device(): lax.all_gather(eig_mine, 'dom', axis=0, tiled=True)]
    all_to_all x1, blocking collectives: 214 us -> 159 us  [on_device(): lax.all_to_all(local_profile, 'ord', split_axis=0, concat_axis=2, tiled=T...]
  transfers between devices with their start and end apart: 2 -> 3, of which waited for: 2 -> 2; matrix products, arithmetic and copies ran while one was open for 0% -> 0% of each run, Pallas kernels for 0% -> 0%
where the time goes in v1:
time: 1150 us
  waiting for transfers between devices  622 us (54%)
  blocking collectives  453 us (39%)
  other arithmetic  25.4 us (2%)
  matrix products  16.1 us (1%)
  between operations  13.6 us (1%)
  starting transfers between devices  12.9 us (1%)
    reduce_scatter x1, waiting for transfers between devices, on_device(): lax.psum_scatter(partial_value, 'dom', scatter_dimension=0, tiled=True)  620 us
    all_gather x1, blocking collectives, on_device(): lax.all_gather(u_mine, 'dom', axis=0, tiled=True)  294 us
    all_to_all x1, blocking collectives, on_device(): lax.all_to_all(local_profile, 'ord', split_axis=0, concat_axis=2, tiled=T...  159 us
  transfers between devices with their start and end apart: 3, of which 2 were waited for; matrix products, arithmetic and copies ran while one was open for 0% of the time, Pallas kernels for 0%

profile of v1, /device:TPU:1, one launch (start us, length us, event | category | flops | bytes accessed | tf_op | source)
XLA Modules:
  0.0 1149.2 jit_solution(14089253161966752242)
XLA Ops:
  6.5 3.0 multiply_convert_fusion.1
  10.4 1.5 convolution_convert_fusion.3
  11.9 1.1 copy.49
  13.0 6.7 all-to-all-start
  19.6 1.4 all-to-all-done
  21.3 6.0 and_select_fusion
  27.4 2.0 copy-done.1
  29.3 1.2 fusion.2
  30.5 4.5 fusion.13
  35.1 620.3 %reduce-scatter.2.cloned.1.call-done = f32[1,128,128]{2,1,0:T(8,128)} async-done(((f32[128,128,128]{2,1,0:T(8,128)}), f32[1,128,128]{2,1,0:T(8,128)}) %reduce-scatter.2.cloned.1.call-update) | async-done | bytes 65552 | tf_op jit(solution)/shard_map/reduce_scatter | solution.py:85
  655.4 1.0 fusion.26
  656.6 1.5 custom-call.12
  658.8 0.6 select_select_fusion.3
  659.4 1.2 custom-call.13
  660.8 1.0 fusion.24
  662.1 1.5 custom-call.14
  664.9 1.2 custom-call.15
  666.3 1.0 fusion.22
  667.5 1.5 custom-call.16
  669.7 0.6 select_select_fusion.1
  670.3 1.2 custom-call.17
  671.8 1.0 fusion.20
  673.0 1.5 custom-call.18
  675.8 1.2 custom-call.19
  677.2 0.9 stack.6
  678.1 6.2 all-to-all-start.1
  684.3 0.9 convolution_convert_fusion.4
  685.2 293.9 %all-gather = bf16[2048,128]{1,0:T(8,128)(2,1)S(1)} all-gather(bf16[16,128]{1,0:T(8,128)(2,1)S(1)} %convolution_convert_fusion.4), channel_id=2, replica_groups=mesh['dom'=128,'ord'=2] {'dom'}, dimensions={0}, use_global_device_ids=true | all-gather | bytes 528384 | tf_op jit(solution)/shard_map/all_gather | solution.py:92
  979.1 1.3 convolution_convert_fusion.1
  980.4 1.3 copy.59
  981.7 158.7 %all_to_all.35 = bf16[8,128,256]{2,1,0:T(8,128)(2,1)S(1)} all-to-all(bf16[8,128,256]{2,1,0:T(8,128)(2,1)S(1)} %copy.59), channel_id=1, replica_groups=mesh['dom'=128,'ord'=2] {'ord'}, dimensions={0} | all-to-all | bytes 1048576 | tf_op jit(solution)/shard_map/all_to_all | solution.py:100
  1141.1 1.2 convolution_convert_fusion
  (44 shorter events, 7.4 us)
Async XLA Ops:
  6.5 648.9 %copy-start = (f32[128,16,128]{2,1,0:T(8,128)S(1)}, f32[128,16,128]{2,1,0:T(8,128)}, u32[]{:S(2)}) copy-start(f32[128,16,128]{2,1,0:T(8,128)} %param.14) | copy-start | bytes 3145732
  6.5 13.1 %copy-start.3 = (s32[128]{0:T(128)S(1)}, s32[128]{0:T(128)}, u32[]{:S(2)}) copy-start(s32[128]{0:T(128)} %param.11) | copy-start | bytes 1540
  6.5 14.7 %copy-start.2 = (s32[128]{0:T(128)S(1)}, s32[128]{0:T(128)}, u32[]{:S(2)}) copy-start(s32[128]{0:T(128)} %param.12) | copy-start | bytes 1540
  13.0 8.1 all-to-all-start
  19.6 635.7 %reduce-scatter.2.cloned.1.call-start = ((), (), s32[]{:S(2)}) async-start(), calls=%async_computation.4 | async-start | bytes 8454144 | tf_op jit(solution)/shard_map/reduce_scatter | solution.py:85
  27.4 2.0 copy-start.1
  678.1 300.9 %all-to-all-start.1 = ((bf16[128,1,16,128]{3,2,1,0:T(8,128)(2,1)}), bf16[128,1,16,128]{3,2,1,0:T(8,128)(2,1)S(1)}, u32[]{:S(2)}, u32[]{:S(2)}) async-start(bf16[128,1,16,128]{3,2,1,0:T(8,128)(2,1)} %stack.6), calls=%async_computation.2 | async-start | bytes 1048576 | tf_op jit(solution)/shard_map/all_to_all | solution.py:17
Sparse Core Ops, SparseCore 0:
  35.2 620.1 reduce-scatter.1
